TPU v7x, 256 devices: a whole 4x4x8 slice. The times are simulated.
256 devices in a mesh: dp: 32 (over x_hi, z, core), tensor: 8 (over y, x_lo).
Axes of the slice: x: 4 (x_hi: 2, x_lo: 2; x = x_hi * 2 + x_lo), y: 4, z: 8, core: 2. Of those that a mesh axis runs over, the one named last changes fastest.
Arguments:
- master: float32 [2, 16384, 16384], P(None, ('tensor', 'dp')), may hold values from -0.1875 to 0.1875
- tile_order: int32 [8, 16], P('tensor'), may hold values from 0 to 15, each once within a row
- check_weights: int32 [8, 16384], P(None, 'tensor'), may hold values from -7 to 7
Outputs:
- tiled: bfloat16 [2, 16384, 16384], P(None, 'tensor', 'dp')
- checksum: float32 [2, 8, 16384], P(None, None, ('dp', 'tensor'))
Inputs may be any that keep to these rules, and one draw needn't show every extreme that they name: Each row of tile_order lists every number of 0 to 15 once.
All inputs are finite; a program needn't handle non-finite values.
Results may differ from a plain program's by a relative error of at most 0.0029.
Values may be sent and summed in bfloat16 or wider, within the bound.
No kernel may reach another device: no remote copies, remote signals or barrier semaphores. Data moves between devices by JAX's collectives and lax.ppermute only.
A program may use at most 128 MiB of HBM per device.

v0:
```python
import jax
import jax.numpy as jnp
from jax import lax
from jax.sharding import PartitionSpec as P

TILE = 128


def on_device(master, tile_order, check_weights):
    tile_rows = TILE
    order = tile_order[0]
    count = order.shape[0]
    low = master.astype(jnp.bfloat16)
    weights = check_weights.astype(jnp.bfloat16)
    received = lax.all_to_all(low, "dp", split_axis=2, concat_axis=1, tiled=True)
    items = received.shape[0]
    columns = received.shape[2]
    blocks = received.reshape(items, count, tile_rows, columns)
    moved = jnp.take(blocks, order, axis=1)
    tiled = moved.reshape(items, count * tile_rows, columns)
    partial_sums = jnp.einsum("cr,lrd->lcd", weights, tiled, preferred_element_type=jnp.float32)
    checksum = lax.psum_scatter(partial_sums, "tensor", scatter_dimension=2, tiled=True)
    return (tiled, checksum)


def solution(mesh):
    in_specs = (P(None, ("tensor", "dp"), None), P("tensor", None), P(None, "tensor"))
    out_specs = (P(None, "tensor", "dp"), P(None, None, ("dp", "tensor")))
    return jax.shard_map(
        on_device, mesh=mesh, in_specs=in_specs, out_specs=out_specs, check_vma=False
    )
```

profile of v0, /device:TPU:4, one launch (start us, length us, event | category | flops | bytes accessed | tf_op | source)
XLA Modules:
  0.0 244.3 jit_solution(6594867219500252485)
XLA Ops:
  7.2 5.9 %convert_element_type.6 = bf16[2,64,16384]{2,1,0:T(8,128)(2,1)} convert(f32[2,64,16384]{2,1,0:T(8,128)} %param.3) | non-fusion elementwise | flops 2097152 | bytes 12582912 | tf_op jit(solution)/shard_map/convert_element_type | solution.py:13
  13.1 17.8 %copy.7 = bf16[2,64,16384]{1,0,2:T(2,128)(2,1)} copy(bf16[2,64,16384]{2,1,0:T(8,128)(2,1)} %convert_element_type.6) | data formatting | bytes 8388608 | tf_op jit(solution)/shard_map/convert_element_type | solution.py:13
  30.9 13.9 %reshape.57 = bf16[32,2,32768]{2,1,0:T(2,128)(2,1)} reshape(bf16[16384,2,64]{2,1,0:T(2,128)(2,1)} %bitcast.26) | data formatting | bytes 8388608
  44.7 0.0 copy-start.2
  44.7 11.8 %all-to-all-start = ((bf16[32,2,32768]{2,1,0:T(2,128)(2,1)}), bf16[32,2,32768]{2,1,0:T(2,128)(2,1)}, u32[]{:S(2)}, u32[]{:S(2)}) async-start(bf16[32,2,32768]{2,1,0:T(2,128)(2,1)} %reshape.57), calls=%async_computation | async-start | bytes 8388608 | tf_op jit(solution)/shard_map/all_to_all | solution.py:15
  56.5 0.0 reduce-scatter.4.cloned.1.call-start
  56.6 0.0 copy-done.2
  56.6 0.1 broadcast_bitcast_fusion
  56.7 93.7 %all-to-all-done = bf16[32,2,32768]{2,1,0:T(2,128)(2,1)} async-done(((bf16[32,2,32768]{2,1,0:T(2,128)(2,1)}), bf16[32,2,32768]{2,1,0:T(2,128)(2,1)}, u32[]{:S(2)}, u32[]{:S(2)}) %all-to-all-start) | async-done | bytes 4194336 | tf_op jit(solution)/shard_map/all_to_all | solution.py:15
  150.3 13.7 %reshape.58 = bf16[16384,2,64]{2,1,0:T(2,128)(2,1)} reshape(bf16[32,2,32768]{2,1,0:T(2,128)(2,1)} %all-to-all-done) | data formatting | bytes 8388608
  164.0 18.5 %copy.12 = bf16[2,64,32,512]{3,1,2,0:T(8,128)(2,1)} copy(bf16[2,64,32,512]{1,0,3,2:T(2,128)(2,1)} %bitcast.27) | data formatting | bytes 8388608 | tf_op jit(solution)/shard_map/all_to_all | solution.py:15
  182.5 4.9 %gather_fusion = bf16[16,2,128,512]{3,2,1,0:T(8,128)(2,1)} fusion(bf16[2,16,128,512]{3,2,1,0:T(8,128)(2,1)} %bitcast.28, s32[1024]{0:T(1024)S(1)} %pad_clamp_fusion), kind=kCustom, calls=%fused_computation | custom fusion | bytes 8388672 | tf_op jit(solution)/shard_map/jit(_take)/gather | solution.py:19
  187.5 2.6 %copy.10 = bf16[2,16,128,512]{3,2,1,0:T(8,128)(2,1)S(1)} copy(bf16[2,16,128,512]{3,2,0,1:T(8,128)(2,1)} %bitcast.29) | data formatting | bytes 8388608 | tf_op jit(solution)/shard_map/jit(_take)/gather | solution.py:19
  190.1 0.0 copy-start.1
  190.1 0.9 bitcast_select_fusion
  191.0 0.0 copy-start
  191.0 2.0 copy-done
  193.0 0.0 copy-done.1
  193.0 0.6 convolution_bitcast_fusion
  193.7 0.3 copy.13
  193.9 1.0 reshape.55
  194.9 0.0 reduce-scatter.4.cloned.1.call-update
  194.9 41.0 %reduce-scatter.4.cloned.1.call-done = f32[64,16]{1,0:T(8,128)} async-done(((f32[512,16]{1,0:T(8,128)}), f32[64,16]{1,0:T(8,128)}) %reduce-scatter.4.cloned.1.call-update) | async-done | bytes 4112
  235.9 0.9 reshape.56
  236.8 0.7 copy.14
  (3 shorter events, 0.0 us)
Async XLA Ops:
  44.7 11.8 %copy-start.2 = (s32[1,16]{1,0:T(1,128)S(1)}, s32[1,16]{1,0:T(1,128)}, u32[]{:S(2)}) copy-start(s32[1,16]{1,0:T(1,128)} %param.4) | copy-start | bytes 196
  44.7 105.6 %all-to-all-start = ((bf16[32,2,32768]{2,1,0:T(2,128)(2,1)}), bf16[32,2,32768]{2,1,0:T(2,128)(2,1)}, u32[]{:S(2)}, u32[]{:S(2)}) async-start(bf16[32,2,32768]{2,1,0:T(2,128)(2,1)} %reshape.57), calls=%async_computation | async-start | bytes 8388608 | tf_op jit(solution)/shard_map/all_to_all | solution.py:15
  56.5 179.4 %reduce-scatter.4.cloned.1.call-start = ((), (), s32[]{:S(2)}) async-start(), calls=%async_computation.2 | async-start | bytes 294912
  190.1 2.9 %copy-start.1 = (s32[8,2048]{1,0:T(8,128)S(1)}, s32[8,2048]{1,0:T(8,128)}, u32[]{:S(2)}) copy-start(s32[8,2048]{1,0:T(8,128)} %param.5) | copy-start | bytes 196612
  191.0 2.0 copy-start
Sparse Core Ops, SparseCore 0:
  195.1 40.8 reduce-scatter.3
where the time goes:
time: 246 us; the launch traced here: 244 us
  waiting for transfers between devices  135 us (55%)
  local copies, waits for them, and re-layouts  76.3 us (31%)
  between operations  14.1 us (6%)
  starting transfers between devices  11.8 us (5%)
  other arithmetic  6.79 us (3%)
    all_to_all x1, waiting for transfers between devices, on_device(): lax.all_to_all(low, 'dp', split_axis=2, concat_axis=1, tiled=True)  93.7 us
    unnamed x2, waiting for transfers between devices  41 us
    unnamed x12, local copies, waits for them, and re-layouts  32.3 us
    all_to_all x1, local copies, waits for them, and re-layouts, on_device(): lax.all_to_all(low, 'dp', split_axis=2, concat_axis=1, tiled=True)  18.5 us
    convert_element_type x1, local copies, waits for them, and re-layouts, on_device(): low = master.astype(jnp.bfloat16)  17.8 us
    all_to_all x1, starting transfers between devices, on_device(): lax.all_to_all(low, 'dp', split_axis=2, concat_axis=1, tiled=True)  11.8 us
    gather x2, local copies, waits for them, and re-layouts, on_device(): moved = jnp.take(blocks, order, axis=1)  7.57 us
    convert_element_type x1, other arithmetic, on_device(): low = master.astype(jnp.bfloat16)  5.9 us
  transfers between devices with their start and end apart: 2, of which 2 were waited for; matrix products, arithmetic and copies ran while one was open for 0% of the time, Pallas kernels for 0%

commit v1 on v0

--- a/solution.py
+++ b/solution.py
@@ -12,7 +12,13 @@
     count = order.shape[0]
     low = master.astype(jnp.bfloat16)
     weights = check_weights.astype(jnp.bfloat16)
-    received = lax.all_to_all(low, "dp", split_axis=2, concat_axis=1, tiled=True)
+    slots_state = lambda sheet: jnp.concatenate(
+        lax.all_to_all(
+            jnp.stack(jnp.split(sheet, lax.axis_size("dp"), axis=2), axis=0), "dp", 0, 0
+        ),
+        axis=1,
+    )
+    received = slots_state(low)
     items = received.shape[0]
     columns = received.shape[2]
     blocks = received.reshape(items, count, tile_rows, columns)

time: 246 us -> 205 us (0.83)
  local copies, waits for them, and re-layouts: 76.3 us -> 38.4 us
    convert_element_type x1 -> x0, local copies, waits for them, and re-layouts: 17.8 us -> none  [on_device(): low = master.astype(jnp.bfloat16)]
    all_to_all x1, local copies, waits for them, and re-layouts: 18.5 us -> 4.7 us  [on_device(): lax.all_to_all(jnp.stack(jnp.split(sheet, lax.axis_size('dp'), axis=2), a...]
    unnamed x12 -> x41, local copies, waits for them, and re-layouts: 32.3 us -> 25.4 us
where the time goes in v1:
time: 205 us; the launch traced here: 204 us
  waiting for transfers between devices  135 us (66%)
  local copies, waits for them, and re-layouts  38.4 us (19%)
  between operations  14.1 us (7%)
  starting transfers between devices  11.8 us (6%)
  other arithmetic  4.76 us (2%)
    all_to_all x1, waiting for transfers between devices, on_device(): lax.all_to_all(jnp.stack(jnp.split(sheet, lax.axis_size('dp'), axis=2), a...  93.7 us
    unnamed x2, waiting for transfers between devices  41 us
    unnamed x41, local copies, waits for them, and re-layouts  25.4 us
    all_to_all x1, starting transfers between devices, on_device(): lax.all_to_all(jnp.stack(jnp.split(sheet, lax.axis_size('dp'), axis=2), a...  11.8 us
    gather x2, local copies, waits for them, and re-layouts, on_device(): moved = jnp.take(blocks, order, axis=1)  7.57 us
    all_to_all x1, local copies, waits for them, and re-layouts, on_device(): lax.all_to_all(jnp.stack(jnp.split(sheet, lax.axis_size('dp'), axis=2), a...  4.7 us
  transfers between devices with their start and end apart: 2, of which 2 were waited for; matrix products, arithmetic and copies ran while one was open for 0% of the time, Pallas kernels for 0%

profile of v1, /device:TPU:4, one launch (start us, length us, event | category | flops | bytes accessed | tf_op | source)
XLA Modules:
  0.0 204.4 jit_solution(17297433592261791428)
XLA Ops:
  7.2 3.9 %convert_element_type.6 = bf16[2,64,16384]{2,1,0:T(8,128)(2,1)S(1)} convert(f32[2,64,16384]{2,1,0:T(8,128)} %param.3) | non-fusion elementwise | flops 2097152 | bytes 12582912 | tf_op jit(solution)/shard_map/convert_element_type | solution.py:13
  11.0 0.7 fusion.31
  11.7 0.7 fusion.30
  12.4 0.7 fusion.29
  13.0 0.7 fusion.28
  13.7 0.7 fusion.27
  14.4 0.7 fusion.26
  15.0 0.7 fusion.25
  15.7 0.7 fusion.24
  16.4 0.7 fusion.23
  17.0 0.7 fusion.22
  17.7 0.7 fusion.21
  18.3 0.7 fusion.20
  19.0 0.7 fusion.19
  19.7 0.7 fusion.18
  20.3 0.7 fusion.17
  21.0 0.7 fusion.16
  21.7 0.7 fusion.15
  22.3 0.7 fusion.14
  23.0 0.7 fusion.13
  23.7 0.7 fusion.12
  24.3 0.7 fusion.11
  25.0 0.7 fusion.10
  25.7 0.7 fusion.9
  26.3 0.7 fusion.8
  27.0 0.7 fusion.7
  27.6 0.7 fusion.6
  28.3 0.7 fusion.5
  29.0 0.7 fusion.4
  29.6 0.7 fusion.3
  30.3 0.7 fusion.2
  31.0 0.7 fusion.1
  31.6 0.7 fusion
  32.3 0.0 copy-start.2
  32.3 11.8 %all-to-all-start = ((bf16[32,2,64,512]{3,2,1,0:T(8,128)(2,1)}), bf16[32,2,64,512]{3,2,1,0:T(8,128)(2,1)}, u32[]{:S(2)}, u32[]{:S(2)}) async-start(bf16[32,2,64,512]{3,2,1,0:T(8,128)(2,1)} %fusion), calls=%async_computation | async-start | bytes 8388608 | tf_op jit(solution)/shard_map/all_to_all | solution.py:16
  44.1 0.0 reduce-scatter.4.cloned.1.call-start
  44.1 0.0 copy-done.2
  44.2 0.1 broadcast_bitcast_fusion
  44.3 93.7 %all-to-all-done = bf16[32,2,64,512]{3,2,1,0:T(8,128)(2,1)} async-done(((bf16[32,2,64,512]{3,2,1,0:T(8,128)(2,1)}), bf16[32,2,64,512]{3,2,1,0:T(8,128)(2,1)}, u32[]{:S(2)}, u32[]{:S(2)}) %all-to-all-start) | async-done | bytes 4194336 | tf_op jit(solution)/shard_map/all_to_all | solution.py:16
  137.9 4.7 %copy.68 = bf16[32,2,64,512]{3,2,0,1:T(8,128)(2,1)} copy(bf16[32,2,64,512]{3,2,1,0:T(8,128)(2,1)} %all-to-all-done) | data formatting | bytes 8388608 | tf_op jit(solution)/shard_map/all_to_all | solution.py:16
  142.6 4.9 %gather_fusion = bf16[16,2,128,512]{3,2,1,0:T(8,128)(2,1)} fusion(bf16[2,16,128,512]{3,2,1,0:T(8,128)(2,1)} %bitcast.150, s32[1024]{0:T(1024)S(1)} %pad_clamp_fusion), kind=kCustom, calls=%fused_computation | custom fusion | bytes 8388672 | tf_op jit(solution)/shard_map/jit(_take)/gather | solution.py:25
  147.6 2.6 %copy.69 = bf16[2,16,128,512]{3,2,1,0:T(8,128)(2,1)S(1)} copy(bf16[2,16,128,512]{3,2,0,1:T(8,128)(2,1)} %bitcast.151) | data formatting | bytes 8388608 | tf_op jit(solution)/shard_map/jit(_take)/gather | solution.py:25
  150.2 0.0 copy-start.1
  150.2 0.9 bitcast_select_fusion
  151.1 0.0 copy-start
  151.1 2.0 copy-done
  153.1 0.0 copy-done.1
  153.1 0.6 convolution_bitcast_fusion
  153.7 0.3 copy.70
  154.0 1.0 reshape.54
  155.0 0.0 reduce-scatter.4.cloned.1.call-update
  155.0 41.0 %reduce-scatter.4.cloned.1.call-done = f32[64,16]{1,0:T(8,128)} async-done(((f32[512,16]{1,0:T(8,128)}), f32[64,16]{1,0:T(8,128)}) %reduce-scatter.4.cloned.1.call-update) | async-done | bytes 4112
  196.0 0.9 reshape.55
  196.9 0.7 copy.71
  (3 shorter events, 0.0 us)
Async XLA Ops:
  32.3 11.8 %copy-start.2 = (s32[1,16]{1,0:T(1,128)S(1)}, s32[1,16]{1,0:T(1,128)}, u32[]{:S(2)}) copy-start(s32[1,16]{1,0:T(1,128)} %param.4) | copy-start | bytes 196
  32.3 105.6 %all-to-all-start = ((bf16[32,2,64,512]{3,2,1,0:T(8,128)(2,1)}), bf16[32,2,64,512]{3,2,1,0:T(8,128)(2,1)}, u32[]{:S(2)}, u32[]{:S(2)}) async-start(bf16[32,2,64,512]{3,2,1,0:T(8,128)(2,1)} %fusion), calls=%async_computation | async-start | bytes 8388608 | tf_op jit(solution)/shard_map/all_to_all | solution.py:16
  44.1 151.9 %reduce-scatter.4.cloned.1.call-start = ((), (), s32[]{:S(2)}) async-start(), calls=%async_computation.2 | async-start | bytes 294912
  150.2 2.9 %copy-start.1 = (s32[8,2048]{1,0:T(8,128)S(1)}, s32[8,2048]{1,0:T(8,128)}, u32[]{:S(2)}) copy-start(s32[8,2048]{1,0:T(8,128)} %param.5) | copy-start | bytes 196612
  151.1 2.0 copy-start
Sparse Core Ops, SparseCore 0:
  155.2 40.8 reduce-scatter.3
